TPU v7x, 128 devices: a whole 4x4x4 slice. The times are simulated.
128 devices in a mesh: dp: 8 (over z, x_hi), tensor: 16 (over y, x_lo, core).
Axes of the slice: x: 4 (x_hi: 2, x_lo: 2; x = x_hi * 2 + x_lo), y: 4, z: 4, core: 2. Of those that a mesh axis runs over, the one named last changes fastest.
Arguments:
- tokens: bfloat16 [4096, 8192], P('dp', 'tensor'), may hold values from -6 to 6
- frozen: bfloat16 [8192, 8192], P('tensor'), may hold values from -0.0625 to 0.0625
- local_param: float32 [64, 128, 128], P('tensor'), may hold values from -0.2 to 0.2
- cross_param: float32 [4, 64, 128, 128], P(None, 'tensor'), may hold values from -0.2 to 0.2
- out_grad: bfloat16 [4096, 8192], P('dp', 'tensor'), may hold values from -0.09375 to 0.09375
Outputs:
- output: float32 [4096, 8192], P('dp', 'tensor')
- local_grad: float32 [64, 128, 128], P('tensor')
- cross_grad: float32 [4, 64, 128, 128], P(None, 'tensor')
All inputs are finite; a program needn't handle non-finite values.
Results may differ from a plain program's by a relative error of at most 0.0029.
Values may be sent and summed in bfloat16 or wider, within the bound.
A program may use at most 192 MiB of HBM per device.

v0:
```python
import jax
import jax.numpy as jnp
from jax import lax
from jax.sharding import PartitionSpec as P


def from_partner(shard, axis, stride):
    return lax.ppermute(shard, axis, [(i, i ^ 1 << stride) for i in range(lax.axis_size(axis))])


def cayley_block(param):
    highest = lax.Precision.HIGHEST
    skew = param - param.T
    identity = jnp.eye(param.shape[0], dtype=param.dtype)
    one_minus = identity - skew
    spd_matrix = identity - jnp.dot(skew, skew, precision=highest)
    numerator = jnp.dot(one_minus, one_minus, precision=highest)
    chol_factor = jnp.linalg.cholesky(spd_matrix)
    return jax.scipy.linalg.cho_solve((chol_factor, True), numerator.T).T


def cayley_many(params):
    return jax.vmap(cayley_block)(params)


def cayley_pull(param, matrix_grad):
    unused, pullback = jax.vjp(cayley_many, param)
    return pullback(matrix_grad)[0]


def split_halves(state, upper_side, blocks_dev, half_block):
    halves = state.reshape(state.shape[0], 2, blocks_dev, half_block)
    own_part = jnp.where(upper_side, halves[:, 1], halves[:, 0])
    other_part = jnp.where(upper_side, halves[:, 0], halves[:, 1])
    return (own_part, other_part)


def join_pair(own_part, received, upper_side):
    low_half = jnp.where(upper_side, received, own_part)
    high_half = jnp.where(upper_side, own_part, received)
    return jnp.concatenate([low_half, high_half], axis=-1)


def split_pair(vector, upper_side, half_block):
    low_half = vector[..., :half_block]
    high_half = vector[..., half_block:]
    keep_part = jnp.where(upper_side, high_half, low_half)
    give_part = jnp.where(upper_side, low_half, high_half)
    return (keep_part, give_part)


def merge_halves(keep_part, returned, upper_side):
    first_half = jnp.where(upper_side, returned, keep_part)
    second_half = jnp.where(upper_side, keep_part, returned)
    return jnp.stack([first_half, second_half], axis=1).reshape(keep_part.shape[0], -1)


def sum_data(value):
    return lax.psum(value, "dp")


def body(tokens, frozen, local_param, cross_param, out_grad):
    highest = lax.Precision.HIGHEST
    token_count, rows_dev = tokens.shape
    block = local_param.shape[-1]
    half_block = block // 2
    blocks_dev = local_param.shape[0]
    levels = lax.axis_size("tensor").bit_length() - 1
    position = lax.axis_index("tensor")
    local_rot = cayley_many(local_param)
    cross_rot = [cayley_many(cross_param[level_idx]) for level_idx in range(levels)]
    inputs = tokens.astype(jnp.float32).reshape(token_count, blocks_dev, block)
    state = jnp.einsum("tci,cij->tcj", inputs, local_rot, precision=highest).reshape(
        token_count, rows_dev
    )
    saved = []
    for level_idx in range(levels):
        upper_side = position >> level_idx & 1 == 1
        own_part, other_part = split_halves(state, upper_side, blocks_dev, half_block)
        received = from_partner(other_part, "tensor", level_idx)
        vector = join_pair(own_part, received, upper_side)
        mixed = jnp.einsum("tci,cij->tcj", vector, cross_rot[level_idx], precision=highest)
        keep_part, give_part = split_pair(mixed, upper_side, half_block)
        returned = from_partner(give_part, "tensor", level_idx)
        state = merge_halves(keep_part, returned, upper_side)
        saved.append(vector)
    rounded = state.astype(jnp.bfloat16)
    partial_out = jnp.dot(rounded, frozen, preferred_element_type=jnp.float32)
    output = lax.psum_scatter(partial_out, "tensor", scatter_dimension=1, tiled=True)
    grad_state = lax.dot_general(
        lax.all_gather(out_grad, "tensor", axis=1, tiled=True),
        frozen,
        (((1,), (1,)), ((), ())),
        preferred_element_type=jnp.float32,
    )
    cross_grads = [None] * levels
    for level_idx in reversed(range(levels)):
        upper_side = position >> level_idx & 1 == 1
        own_part, other_part = split_halves(grad_state, upper_side, blocks_dev, half_block)
        received = from_partner(other_part, "tensor", level_idx)
        grad_vector = join_pair(own_part, received, upper_side)
        matrix_grad = jnp.einsum("tci,tcj->cij", saved[level_idx], grad_vector, precision=highest)
        back_vector = jnp.einsum(
            "tcj,cij->tci", grad_vector, cross_rot[level_idx], precision=highest
        )
        keep_part, give_part = split_pair(back_vector, upper_side, half_block)
        returned = from_partner(give_part, "tensor", level_idx)
        grad_state = merge_halves(keep_part, returned, upper_side)
        param_grad = cayley_pull(cross_param[level_idx], matrix_grad)
        param_grad = sum_data(param_grad)
        cross_grads[level_idx] = param_grad
    grad_blocks = grad_state.reshape(token_count, blocks_dev, block)
    local_matrix = jnp.einsum("tci,tcj->cij", inputs, grad_blocks, precision=highest)
    local_grad = cayley_pull(local_param, local_matrix)
    local_grad = sum_data(local_grad)
    cross_grad = jnp.stack(cross_grads)
    return (output, local_grad, cross_grad)


def solution(mesh):
    in_specs = (
        P("dp", "tensor"),
        P("tensor", None),
        P("tensor", None, None),
        P(None, "tensor", None, None),
        P("dp", "tensor"),
    )
    out_specs = (P("dp", "tensor"), P("tensor", None, None), P(None, "tensor", None, None))
    return jax.shard_map(body, mesh=mesh, in_specs=in_specs, out_specs=out_specs, check_vma=False)
```

profile of v0, /device:TPU:0, one launch (start us, length us, event | category | flops | bytes accessed | tf_op | source)
XLA Modules:
  0.0 1785.8 jit_solution(9196138787854236795)
XLA Ops:
  24.3 48.0 %custom-call.110 = f32[4,128,128]{2,1,0:T(8,128)} custom-call(f32[4,128,128]{2,1,0:T(8,128)S(1)} %copy.622), custom_call_target="Cholesky" | custom-call | tf_op jit(solution)/shard_map/vmap(jit(cholesky))/cholesky/custom-call.1 | solution.py:18
  73.4 47.5 %custom-call.101 = f32[4,128,128]{2,1,0:T(8,128)} custom-call(f32[4,128,128]{2,1,0:T(8,128)S(1)} %copy.595), custom_call_target="Cholesky" | custom-call | tf_op jit(solution)/shard_map/vmap(jit(cholesky))/cholesky/custom-call.1 | solution.py:18
  122.1 47.5 %custom-call.104 = f32[4,128,128]{2,1,0:T(8,128)} custom-call(f32[4,128,128]{2,1,0:T(8,128)S(1)} %copy.604), custom_call_target="Cholesky" | custom-call | tf_op jit(solution)/shard_map/vmap(jit(cholesky))/cholesky/custom-call.1 | solution.py:18
  170.7 47.7 %custom-call.107 = f32[4,128,128]{2,1,0:T(8,128)} custom-call(f32[4,128,128]{2,1,0:T(8,128)S(1)} %copy.613), custom_call_target="Cholesky" | custom-call | tf_op jit(solution)/shard_map/vmap(jit(cholesky))/cholesky/custom-call.1 | solution.py:18
  219.5 47.6 %custom-call.98 = f32[4,128,128]{2,1,0:T(8,128)} custom-call(f32[4,128,128]{2,1,0:T(8,128)S(1)} %copy.586), custom_call_target="Cholesky" | custom-call | tf_op jit(solution)/shard_map/vmap(jit(cholesky))/cholesky/custom-call.1 | solution.py:18
  267.2 46.9 %custom-call.113 = f32[4,128,128]{2,1,0:T(8,128)S(1)} custom-call(f32[4,128,128]{2,1,0:T(8,128)S(1)} %fusion.150), custom_call_target="Cholesky" | custom-call | tf_op jit(solution)/shard_map/jvp(vmap(jit(cholesky)))/cholesky/custom-call.1 | solution.py:18
  319.2 47.9 %custom-call.131 = f32[4,128,128]{2,1,0:T(8,128)S(1)} custom-call(f32[4,128,128]{2,1,0:T(8,128)} %get-tuple-element.209), custom_call_target="Cholesky" | custom-call | tf_op jit(solution)/shard_map/jvp(vmap(jit(cholesky)))/cholesky/custom-call.1 | solution.py:18
  367.2 46.9 %custom-call.122 = f32[4,128,128]{2,1,0:T(8,128)S(1)} custom-call(f32[4,128,128]{2,1,0:T(8,128)S(1)} %get-tuple-element.210), custom_call_target="Cholesky" | custom-call | tf_op jit(solution)/shard_map/jvp(vmap(jit(cholesky)))/cholesky/custom-call.1 | solution.py:18
  417.0 46.9 %custom-call.149 = f32[4,128,128]{2,1,0:T(8,128)S(1)} custom-call(f32[4,128,128]{2,1,0:T(8,128)S(1)} %get-tuple-element.207), custom_call_target="Cholesky" | custom-call | tf_op jit(solution)/shard_map/jvp(vmap(jit(cholesky)))/cholesky/custom-call.1 | solution.py:18
  463.9 48.1 %custom-call.140 = f32[4,128,128]{2,1,0:T(8,128)S(1)} custom-call(f32[4,128,128]{2,1,0:T(8,128)} %get-tuple-element.208), custom_call_target="Cholesky" | custom-call | tf_op jit(solution)/shard_map/jvp(vmap(jit(cholesky)))/cholesky/custom-call.1 | solution.py:18
  518.0 39.3 %custom-call.112 = f32[4,1,128,128]{2,3,1,0:T(8,128)S(1)} custom-call(f32[4,1,128,128]{3,2,1,0:T(8,128)S(1)} %get-tuple-element.200), custom_call_target="InvertDiagBlocksLowerTriangular" | custom-call | tf_op jit(solution)/shard_map/vmap(jit(_cho_solve))/triangular_solve/custom-call.2 | solution.py:19
  569.4 40.9 %custom-call.100 = f32[4,1,128,128]{2,3,1,0:T(8,128)} custom-call(f32[4,1,128,128]{3,2,1,0:T(8,128)} %select_bitcast_fusion.13), custom_call_target="InvertDiagBlocksLowerTriangular" | custom-call | tf_op jit(solution)/shard_map/vmap(jit(_cho_solve))/triangular_solve/custom-call.2 | solution.py:19
  610.3 40.8 %custom-call.109 = f32[4,1,128,128]{2,3,1,0:T(8,128)} custom-call(f32[4,1,128,128]{3,2,1,0:T(8,128)} %get-tuple-element.199), custom_call_target="InvertDiagBlocksLowerTriangular" | custom-call | tf_op jit(solution)/shard_map/vmap(jit(_cho_solve))/triangular_solve/custom-call.2 | solution.py:19
  667.8 40.1 %custom-call.152 = f32[4,1,128,128]{2,3,1,0:T(8,128)S(1)} custom-call(f32[4,1,128,128]{3,2,1,0:T(8,128)} %get-tuple-element.195), custom_call_target="InvertDiagBlocksLowerTriangular" | custom-call | tf_op jit(solution)/shard_map/transpose(jvp(vmap(jit(_cho_solve))))/triangular_solve/custom-call.0 | solution.py:19
  721.6 40.2 %custom-call.106 = f32[4,1,128,128]{2,3,1,0:T(8,128)S(1)} custom-call(f32[4,1,128,128]{3,2,1,0:T(8,128)} %get-tuple-element.198), custom_call_target="InvertDiagBlocksLowerTriangular" | custom-call | tf_op jit(solution)/shard_map/vmap(jit(_cho_solve))/triangular_solve/custom-call.2 | solution.py:19
  774.6 40.1 %custom-call.116 = f32[4,1,128,128]{2,3,1,0:T(8,128)S(1)} custom-call(f32[4,1,128,128]{3,2,1,0:T(8,128)} %get-tuple-element.201), custom_call_target="InvertDiagBlocksLowerTriangular" | custom-call | tf_op jit(solution)/shard_map/transpose(jvp(vmap(jit(_cho_solve))))/triangular_solve/custom-call.0 | solution.py:19
  814.7 40.7 %custom-call.143 = f32[4,1,128,128]{2,3,1,0:T(8,128)} custom-call(f32[4,1,128,128]{3,2,1,0:T(8,128)} %get-tuple-element.203), custom_call_target="InvertDiagBlocksLowerTriangular" | custom-call | tf_op jit(solution)/shard_map/transpose(jvp(vmap(jit(_cho_solve))))/triangular_solve/custom-call.0 | solution.py:19
  855.4 40.1 %custom-call.134 = f32[4,1,128,128]{2,3,1,0:T(8,128)S(1)} custom-call(f32[4,1,128,128]{3,2,1,0:T(8,128)} %get-tuple-element.205), custom_call_target="InvertDiagBlocksLowerTriangular" | custom-call | tf_op jit(solution)/shard_map/transpose(jvp(vmap(jit(_cho_solve))))/triangular_solve/custom-call.0 | solution.py:19
  912.7 40.1 %custom-call.125 = f32[4,1,128,128]{2,3,1,0:T(8,128)S(1)} custom-call(f32[4,1,128,128]{3,2,1,0:T(8,128)} %get-tuple-element.173), custom_call_target="InvertDiagBlocksLowerTriangular" | custom-call | tf_op jit(solution)/shard_map/transpose(jvp(vmap(jit(_cho_solve))))/triangular_solve/custom-call.0 | solution.py:19
  952.8 40.1 %custom-call.103 = f32[4,1,128,128]{2,3,1,0:T(8,128)S(1)} custom-call(f32[4,1,128,128]{3,2,1,0:T(8,128)} %get-tuple-element.197), custom_call_target="InvertDiagBlocksLowerTriangular" | custom-call | tf_op jit(solution)/shard_map/vmap(jit(_cho_solve))/triangular_solve/custom-call.2 | solution.py:19
  1012.8 7.4 collective-permute-done.5
  1032.8 40.8 %custom-call.129 = f32[4,1,128,128]{2,3,1,0:T(8,128)} custom-call(f32[4,1,128,128]{3,2,1,0:T(8,128)} %get-tuple-element.172), custom_call_target="InvertDiagBlocksLowerTriangular" | custom-call | tf_op jit(solution)/shard_map/transpose(jvp(vmap(jit(cholesky))))/triangular_solve/custom-call.2 | solution.py:18
  1073.6 40.7 %custom-call.156 = f32[4,1,128,128]{2,3,1,0:T(8,128)} custom-call(f32[4,1,128,128]{3,2,1,0:T(8,128)} %get-tuple-element.196), custom_call_target="InvertDiagBlocksLowerTriangular" | custom-call | tf_op jit(solution)/shard_map/transpose(jvp(vmap(jit(cholesky))))/triangular_solve/custom-call.2 | solution.py:18
  1114.3 40.7 %custom-call.120 = f32[4,1,128,128]{2,3,1,0:T(8,128)} custom-call(f32[4,1,128,128]{3,2,1,0:T(8,128)} %get-tuple-element.202), custom_call_target="InvertDiagBlocksLowerTriangular" | custom-call | tf_op jit(solution)/shard_map/transpose(jvp(vmap(jit(cholesky))))/triangular_solve/custom-call.2 | solution.py:18
  1155.1 40.7 %custom-call.147 = f32[4,1,128,128]{2,3,1,0:T(8,128)} custom-call(f32[4,1,128,128]{3,2,1,0:T(8,128)} %get-tuple-element.204), custom_call_target="InvertDiagBlocksLowerTriangular" | custom-call | tf_op jit(solution)/shard_map/transpose(jvp(vmap(jit(cholesky))))/triangular_solve/custom-call.2 | solution.py:18
  1195.8 41.1 %custom-call.138 = f32[4,1,128,128]{2,3,1,0:T(8,128)} custom-call(f32[4,1,128,128]{3,2,1,0:T(8,128)} %get-tuple-element.206), custom_call_target="InvertDiagBlocksLowerTriangular" | custom-call | tf_op jit(solution)/shard_map/transpose(jvp(vmap(jit(cholesky))))/triangular_solve/custom-call.2 | solution.py:18
  1248.8 9.4 fusion.288
  1273.8 7.4 collective-permute-done.8
  1321.2 4.8 collective-permute-done.10
  1498.5 11.7 fusion.287
  1510.2 83.0 %all-reduce.3.cloned.1.call-done = (f32[4,128,128]{2,1,0:T(8,128)}, f32[1,4,128,128]{3,2,1,0:T(8,128)}, f32[1,4,128,128]{3,2,1,0:T(8,128)}, f32[1,4,128,128]{3,2,1,0:T(8,128)}, f32[1,4,128,128]{3,2,1,0:T(8,128)}) async-done(((f32[4,128,128]{2,1,0:T(8,128)}, f32[1,4,128,128]{3,2,1,0:T(8,128)}, f32[1,4,128,128]{3,2,1,0:T(8,128)}, f32[1,4,128,128]{3,2,1,0:T(8,128)}, f32[1,4,128,128]{3,2,1,0:T(8,128)}), ...) | async-done | bytes 1310736 | tf_op jit(solution)/shard_map/psum | solution.py:59
  1595.4 182.0 %reduce-scatter.2.cloned.1.call-done = f32[512,512]{1,0:T(8,128)} async-done(((f32[512,8192]{1,0:T(8,128)}), f32[512,512]{1,0:T(8,128)}) %reduce-scatter.2.cloned.1.call-update) | async-done | bytes 1048592 | tf_op jit(solution)/shard_map/reduce_scatter | solution.py:89
  (376 shorter events, 383.0 us)
Async XLA Ops:
  7.2 551.7 %copy-start = (bf16[512,512]{1,0:T(8,128)(2,1)S(1)}, bf16[512,512]{1,0:T(8,128)(2,1)}, u32[]{:S(2)}) copy-start(bf16[512,512]{1,0:T(8,128)(2,1)} %param.24) | copy-start | bytes 1572868
  7.2 1241.6 %all-gather.2.cloned.1.call-start = ((), (), s32[]{:S(2)}) async-start(), calls=%async_computation.2 | async-start | bytes 8912896 | tf_op jit(solution)/shard_map/all_gather | solution.py:91
  7.9 1585.2 %all-reduce.3.cloned.1.call-start = ((), (), s32[]{:S(2)}) async-start(), calls=%async_computation.3 | async-start | bytes 2621440 | tf_op jit(solution)/shard_map/psum | solution.py:59
  314.1 245.4 %copy-start.40 = (f32[4,128,128]{2,1,0:T(8,128)}, f32[4,128,128]{2,1,0:T(8,128)S(1)}, u32[]{:S(2)}) copy-start(f32[4,128,128]{2,1,0:T(8,128)S(1)} %custom-call.113) | copy-start | bytes 786436
  367.1 192.3 %copy-start.43 = (f32[4,128,128]{2,1,0:T(8,128)}, f32[4,128,128]{2,1,0:T(8,128)S(1)}, u32[]{:S(2)}) copy-start(f32[4,128,128]{2,1,0:T(8,128)S(1)} %custom-call.131) | copy-start | bytes 786436
  414.1 143.3 %copy-start.41 = (f32[4,128,128]{2,1,0:T(8,128)}, f32[4,128,128]{2,1,0:T(8,128)S(1)}, u32[]{:S(2)}) copy-start(f32[4,128,128]{2,1,0:T(8,128)S(1)} %custom-call.122) | copy-start | bytes 786436
  463.9 54.1 %copy-start.45 = (f32[4,128,128]{2,1,0:T(8,128)}, f32[4,128,128]{2,1,0:T(8,128)S(1)}, u32[]{:S(2)}) copy-start(f32[4,128,128]{2,1,0:T(8,128)S(1)} %custom-call.149) | copy-start | bytes 786436
  512.0 47.4 %copy-start.44 = (f32[4,128,128]{2,1,0:T(8,128)}, f32[4,128,128]{2,1,0:T(8,128)S(1)}, u32[]{:S(2)}) copy-start(f32[4,128,128]{2,1,0:T(8,128)S(1)} %custom-call.140) | copy-start | bytes 786436
  566.5 88.1 %collective-permute-start = (f32[512,4,64]{0,2,1:T(8,128)}, f32[512,4,64]{0,2,1:T(8,128)}, u32[]{:S(2)}, u32[]{:S(2)}) collective-permute-start(f32[512,4,64]{0,2,1:T(8,128)} %copy.630), channel_id=1, source_target_pairs={{0,1},{1,0},{2,3},{3,2},{4,5},{5,4},{6,7},{7,6},{8,9},{9,8},{10,11... | collective-permute-start | bytes 1572872 | tf_op jit(solution)/shard_map/ppermute | solution.py:8
  567.5 98.0 %copy-start.22 = (f32[4,128,128]{2,1,0:T(8,128)}, f32[4,128,128]{2,1,0:T(8,128)S(1)}, u32[]{:S(2)}) copy-start(f32[4,128,128]{2,1,0:T(8,128)S(1)} %fusion.189) | copy-start | bytes 786436
  665.5 46.0 %collective-permute-start.1 = (f32[512,4,64]{0,2,1:T(8,128)}, f32[512,4,64]{0,2,1:T(8,128)}, u32[]{:S(2)}, u32[]{:S(2)}) collective-permute-start(f32[512,4,64]{0,2,1:T(8,128)} %copy.634), channel_id=1, source_target_pairs={{0,1},{1,0},{2,3},{3,2},{4,5},{5,4},{6,7},{7,6},{8,9},{9,8},{10,11... | collective-permute-start | bytes 1572872 | tf_op jit(solution)/shard_map/ppermute | solution.py:8
  707.9 58.4 %copy-start.2 = (f32[4,1,128,128]{2,3,1,0:T(8,128)}, f32[4,1,128,128]{2,3,1,0:T(8,128)S(1)}, u32[]{:S(2)}) copy-start(f32[4,1,128,128]{2,3,1,0:T(8,128)S(1)} %custom-call.152) | copy-start | bytes 786436
  718.7 44.8 %collective-permute-start.2 = (f32[512,4,64]{0,2,1:T(8,128)S(1)}, f32[512,4,64]{0,2,1:T(8,128)}, u32[]{:S(2)}, u32[]{:S(2)}) collective-permute-start(f32[512,4,64]{0,2,1:T(8,128)S(1)} %copy.637), channel_id=1, source_target_pairs={{0,2},{1,3},{2,0},{3,1},{4,6},{5,7},{6,4},{7,5},{8,10},{9,11},{10,... | collective-permute-start | bytes 1572872 | tf_op jit(solution)/shard_map/ppermute | solution.py:8
  721.6 53.0 %copy-start.24 = (f32[4,128,128]{2,1,0:T(8,128)}, f32[4,128,128]{2,1,0:T(8,128)S(1)}, u32[]{:S(2)}) copy-start(f32[4,128,128]{2,1,0:T(8,128)S(1)} %fusion.194) | copy-start | bytes 786436
  773.1 127.1 %collective-permute-start.3 = (f32[512,4,64]{0,2,1:T(8,128)}, f32[512,4,64]{0,2,1:T(8,128)}, u32[]{:S(2)}, u32[]{:S(2)}) collective-permute-start(f32[512,4,64]{0,2,1:T(8,128)} %copy.641), channel_id=1, source_target_pairs={{0,2},{1,3},{2,0},{3,1},{4,6},{5,7},{6,4},{7,5},{8,10},{9,11},{10,... | collective-permute-start | bytes 1572872 | tf_op jit(solution)/shard_map/ppermute | solution.py:8
  895.6 104.1 %copy-start.1 = (f32[4,1,128,128]{2,3,1,0:T(8,128)}, f32[4,1,128,128]{2,3,1,0:T(8,128)S(1)}, u32[]{:S(2)}) copy-start(f32[4,1,128,128]{2,3,1,0:T(8,128)S(1)} %custom-call.134) | copy-start | bytes 786436
  908.1 87.5 %collective-permute-start.4 = (f32[512,4,64]{0,2,1:T(8,128)}, f32[512,4,64]{0,2,1:T(8,128)}, u32[]{:S(2)}, u32[]{:S(2)}) collective-permute-start(f32[512,4,64]{0,2,1:T(8,128)} %copy.644), channel_id=1, source_target_pairs={{0,4},{1,5},{2,6},{3,7},{4,0},{5,1},{6,2},{7,3},{8,12},{9,13},{10,... | collective-permute-start | bytes 1572872 | tf_op jit(solution)/shard_map/ppermute | solution.py:8
  1006.4 13.8 collective-permute-start.5
  1027.4 213.8 %collective-permute-start.6 = (f32[512,4,64]{0,2,1:T(8,128)S(1)}, f32[512,4,64]{0,2,1:T(8,128)}, u32[]{:S(2)}, u32[]{:S(2)}) collective-permute-start(f32[512,4,64]{0,2,1:T(8,128)S(1)} %copy.651), channel_id=1, source_target_pairs={{0,8},{1,9},{2,10},{3,11},{4,12},{5,13},{6,14},{7,15},{8,0},{9,1},... | collective-permute-start | bytes 1572872 | tf_op jit(solution)/shard_map/ppermute | solution.py:8
  1248.2 22.8 %collective-permute-start.7 = (bf16[512,4,64]{0,2,1:T(8,128)(2,1)}, bf16[512,4,64]{0,2,1:T(8,128)(2,1)}, u32[]{:S(2)}, u32[]{:S(2)}) collective-permute-start(bf16[512,4,64]{0,2,1:T(8,128)(2,1)} %copy.655), channel_id=1, source_target_pairs={{0,8},{1,9},{2,10},{3,11},{4,12},{5,13},{6,14},{7,15},{8,0},{9,1},... | collective-permute-start | bytes 786440 | tf_op jit(solution)/shard_map/ppermute | solution.py:8
  1267.4 13.9 collective-permute-start.8
  1293.1 14.8 collective-permute-start.9
  1315.1 11.0 collective-permute-start.10
  1339.3 12.1 collective-permute-start.11
  1359.5 10.2 collective-permute-start.12
  1388.3 9.5 collective-permute-start.13
  1405.8 8.0 collective-permute-start.14
  1431.0 9.6 collective-permute-start.15
  1453.8 19.1 %copy-start.26 = (f32[4,128,128]{2,1,0:T(8,128)S(1)}, f32[4,128,128]{2,1,0:T(8,128)}, u32[]{:S(2)}) copy-start(f32[4,128,128]{2,1,0:T(8,128)} %copy-done.25) | copy-start | bytes 786436
  1472.9 20.9 %copy-start.31 = (f32[4,128,128]{2,1,0:T(8,128)S(1)}, f32[4,128,128]{2,1,0:T(8,128)}, u32[]{:S(2)}) copy-start(f32[4,128,128]{2,1,0:T(8,128)} %copy-done.30) | copy-start | bytes 786436
  1475.2 21.0 %copy-start.32 = (f32[4,128,128]{2,1,0:T(8,128)S(1)}, f32[4,128,128]{2,1,0:T(8,128)}, u32[]{:S(2)}) copy-start(f32[4,128,128]{2,1,0:T(8,128)} %fusion.136) | copy-start | bytes 786436
  1498.4 279.0 %reduce-scatter.2.cloned.1.call-start = ((), (), s32[]{:S(2)}) async-start(), calls=%async_computation.1 | async-start | bytes 17825792 | tf_op jit(solution)/shard_map/reduce_scatter | solution.py:89
  (34 other events, 174.8 us)
Sparse Core Ops, SparseCore 0:
  9.7 54.5 all-gather.1
  1498.5 94.5 all-reduce.2
  1596.1 181.2 reduce-scatter.1
where the time goes:
time: 1800 us; the launch traced here: 1790 us
  other arithmetic  1160 us (64%)
  waiting for transfers between devices  289 us (16%)
  matrix products  186 us (10%)
  local copies, waits for them, and re-layouts  117 us (6%)
  starting transfers between devices  20.2 us (1%)
    another operation x28, other arithmetic, cayley_block(): chol_factor = jnp.linalg.cholesky(spd_matrix)  685 us
    another operation x11, other arithmetic, cayley_block(): return jax.scipy.linalg.cho_solve((chol_factor, True), numerator.T).T  404 us
    reduce_scatter x1, waiting for transfers between devices, body(): lax.psum_scatter(partial_out, 'tensor', scatter_dimension=1, tiled=True)  182 us
    psum x1, waiting for transfers between devices, sum_data(): return lax.psum(value, 'dp')  83 us
    another operation x40, matrix products, cayley_block(): return jax.scipy.linalg.cho_solve((chol_factor, True), numerator.T).T  58.6 us
  transfers between devices with their start and end apart: 19, of which 7 were waited for; matrix products, arithmetic and copies ran while one was open for 73% of the time, Pallas kernels for 0%

commit v1 on v0

--- a/solution.py
+++ b/solution.py
@@ -56,7 +56,7 @@
 
 
 def sum_data(value):
-    return lax.psum(value, "dp")
+    return jnp.sum(lax.all_gather(value, "dp"), axis=0)
 
 
 def body(tokens, frozen, local_param, cross_param, out_grad):

time: 1800 us -> 1940 us (1.078)
  waiting for transfers between devices: 289 us -> 421 us
    all_gather x0 -> x5, waiting for transfers between devices: none -> 211 us  [sum_data(): return jnp.sum(lax.all_gather(value, 'dp'), axis=0)]
    psum x1 -> x0, waiting for transfers between devices: 83 us -> none  [sum_data(): return lax.psum(value, 'dp')]
  transfers between devices with their start and end apart: 19 -> 23, of which waited for: 7 -> 13; matrix products, arithmetic and copies ran while one was open for 73% -> 70% of each run, Pallas kernels for 0% -> 0%
where the time goes in v1:
time: 1940 us; the launch traced here: 1930 us
  other arithmetic  1170 us (60%)
  waiting for transfers between devices  421 us (22%)
  matrix products  184 us (9%)
  local copies, waits for them, and re-layouts  114 us (6%)
  starting transfers between devices  21.7 us (1%)
    another operation x28, other arithmetic, cayley_block(): chol_factor = jnp.linalg.cholesky(spd_matrix)  686 us
    another operation x11, other arithmetic, cayley_block(): return jax.scipy.linalg.cho_solve((chol_factor, True), numerator.T).T  407 us
    all_gather x5, waiting for transfers between devices, sum_data(): return jnp.sum(lax.all_gather(value, 'dp'), axis=0)  211 us
    reduce_scatter x1, waiting for transfers between devices, body(): lax.psum_scatter(partial_out, 'tensor', scatter_dimension=1, tiled=True)  180 us
    another operation x40, matrix products, cayley_block(): return jax.scipy.linalg.cho_solve((chol_factor, True), numerator.T).T  61.9 us
  transfers between devices with their start and end apart: 23, of which 13 were waited for; matrix products, arithmetic and copies ran while one was open for 70% of the time, Pallas kernels for 0%

profile of v1, /device:TPU:0, one launch (start us, length us, event | category | flops | bytes accessed | tf_op | source)
XLA Modules:
  0.0 1928.3 jit_solution(12291582375116463153)
XLA Ops:
  24.4 47.4 %custom-call.110 = f32[4,128,128]{2,1,0:T(8,128)S(1)} custom-call(f32[4,128,128]{2,1,0:T(8,128)S(1)} %copy.586), custom_call_target="Cholesky" | custom-call | tf_op jit(solution)/shard_map/vmap(jit(cholesky))/cholesky/custom-call.1 | solution.py:18
  72.9 47.5 %custom-call.101 = f32[4,128,128]{2,1,0:T(8,128)} custom-call(f32[4,128,128]{2,1,0:T(8,128)S(1)} %copy.559), custom_call_target="Cholesky" | custom-call | tf_op jit(solution)/shard_map/vmap(jit(cholesky))/cholesky/custom-call.1 | solution.py:18
  121.6 47.5 %custom-call.104 = f32[4,128,128]{2,1,0:T(8,128)} custom-call(f32[4,128,128]{2,1,0:T(8,128)S(1)} %copy.568), custom_call_target="Cholesky" | custom-call | tf_op jit(solution)/shard_map/vmap(jit(cholesky))/cholesky/custom-call.1 | solution.py:18
  170.2 47.7 %custom-call.107 = f32[4,128,128]{2,1,0:T(8,128)} custom-call(f32[4,128,128]{2,1,0:T(8,128)S(1)} %copy.577), custom_call_target="Cholesky" | custom-call | tf_op jit(solution)/shard_map/vmap(jit(cholesky))/cholesky/custom-call.1 | solution.py:18
  219.0 47.6 %custom-call.98 = f32[4,128,128]{2,1,0:T(8,128)} custom-call(f32[4,128,128]{2,1,0:T(8,128)S(1)} %copy.550), custom_call_target="Cholesky" | custom-call | tf_op jit(solution)/shard_map/vmap(jit(cholesky))/cholesky/custom-call.1 | solution.py:18
  266.7 46.9 %custom-call.113 = f32[4,128,128]{2,1,0:T(8,128)S(1)} custom-call(f32[4,128,128]{2,1,0:T(8,128)S(1)} %fusion.146), custom_call_target="Cholesky" | custom-call | tf_op jit(solution)/shard_map/jvp(vmap(jit(cholesky)))/cholesky/custom-call.1 | solution.py:18
  318.9 47.9 %custom-call.131 = f32[4,128,128]{2,1,0:T(8,128)S(1)} custom-call(f32[4,128,128]{2,1,0:T(8,128)} %get-tuple-element.204), custom_call_target="Cholesky" | custom-call | tf_op jit(solution)/shard_map/jvp(vmap(jit(cholesky)))/cholesky/custom-call.1 | solution.py:18
  366.8 47.8 %custom-call.122 = f32[4,128,128]{2,1,0:T(8,128)S(1)} custom-call(f32[4,128,128]{2,1,0:T(8,128)} %get-tuple-element.205), custom_call_target="Cholesky" | custom-call | tf_op jit(solution)/shard_map/jvp(vmap(jit(cholesky)))/cholesky/custom-call.1 | solution.py:18
  417.6 47.7 %custom-call.149 = f32[4,128,128]{2,1,0:T(8,128)S(1)} custom-call(f32[4,128,128]{2,1,0:T(8,128)} %get-tuple-element.202), custom_call_target="Cholesky" | custom-call | tf_op jit(solution)/shard_map/jvp(vmap(jit(cholesky)))/cholesky/custom-call.1 | solution.py:18
  465.3 48.1 %custom-call.140 = f32[4,128,128]{2,1,0:T(8,128)S(1)} custom-call(f32[4,128,128]{2,1,0:T(8,128)} %get-tuple-element.203), custom_call_target="Cholesky" | custom-call | tf_op jit(solution)/shard_map/jvp(vmap(jit(cholesky)))/cholesky/custom-call.1 | solution.py:18
  519.4 40.2 %custom-call.112 = f32[4,1,128,128]{2,3,1,0:T(8,128)S(1)} custom-call(f32[4,1,128,128]{3,2,1,0:T(8,128)} %get-tuple-element.195), custom_call_target="InvertDiagBlocksLowerTriangular" | custom-call | tf_op jit(solution)/shard_map/vmap(jit(_cho_solve))/triangular_solve/custom-call.2 | solution.py:19
  570.8 40.9 %custom-call.100 = f32[4,1,128,128]{2,3,1,0:T(8,128)} custom-call(f32[4,1,128,128]{3,2,1,0:T(8,128)} %select_bitcast_fusion.13), custom_call_target="InvertDiagBlocksLowerTriangular" | custom-call | tf_op jit(solution)/shard_map/vmap(jit(_cho_solve))/triangular_solve/custom-call.2 | solution.py:19
  616.2 40.8 %custom-call.109 = f32[4,1,128,128]{2,3,1,0:T(8,128)} custom-call(f32[4,1,128,128]{3,2,1,0:T(8,128)} %get-tuple-element.194), custom_call_target="InvertDiagBlocksLowerTriangular" | custom-call | tf_op jit(solution)/shard_map/vmap(jit(_cho_solve))/triangular_solve/custom-call.2 | solution.py:19
  672.7 40.9 %custom-call.152 = f32[4,1,128,128]{2,3,1,0:T(8,128)} custom-call(f32[4,1,128,128]{3,2,1,0:T(8,128)} %get-tuple-element.190), custom_call_target="InvertDiagBlocksLowerTriangular" | custom-call | tf_op jit(solution)/shard_map/transpose(jvp(vmap(jit(_cho_solve))))/triangular_solve/custom-call.0 | solution.py:19
  713.6 40.1 %custom-call.116 = f32[4,1,128,128]{2,3,1,0:T(8,128)S(1)} custom-call(f32[4,1,128,128]{3,2,1,0:T(8,128)} %get-tuple-element.196), custom_call_target="InvertDiagBlocksLowerTriangular" | custom-call | tf_op jit(solution)/shard_map/transpose(jvp(vmap(jit(_cho_solve))))/triangular_solve/custom-call.0 | solution.py:19
  753.7 40.1 %custom-call.134 = f32[4,1,128,128]{2,3,1,0:T(8,128)S(1)} custom-call(f32[4,1,128,128]{3,2,1,0:T(8,128)} %get-tuple-element.200), custom_call_target="InvertDiagBlocksLowerTriangular" | custom-call | tf_op jit(solution)/shard_map/transpose(jvp(vmap(jit(_cho_solve))))/triangular_solve/custom-call.0 | solution.py:19
  810.2 40.4 %custom-call.106 = f32[4,1,128,128]{2,3,1,0:T(8,128)S(1)} custom-call(f32[4,1,128,128]{3,2,1,0:T(8,128)} %get-tuple-element.193), custom_call_target="InvertDiagBlocksLowerTriangular" | custom-call | tf_op jit(solution)/shard_map/vmap(jit(_cho_solve))/triangular_solve/custom-call.2 | solution.py:19
  863.9 41.2 %custom-call.125 = f32[4,1,128,128]{2,3,1,0:T(8,128)} custom-call(f32[4,1,128,128]{3,2,1,0:T(8,128)} %get-tuple-element.168), custom_call_target="InvertDiagBlocksLowerTriangular" | custom-call | tf_op jit(solution)/shard_map/transpose(jvp(vmap(jit(_cho_solve))))/triangular_solve/custom-call.0 | solution.py:19
  905.0 40.7 %custom-call.143 = f32[4,1,128,128]{2,3,1,0:T(8,128)} custom-call(f32[4,1,128,128]{3,2,1,0:T(8,128)} %get-tuple-element.198), custom_call_target="InvertDiagBlocksLowerTriangular" | custom-call | tf_op jit(solution)/shard_map/transpose(jvp(vmap(jit(_cho_solve))))/triangular_solve/custom-call.0 | solution.py:19
  945.8 40.7 %custom-call.103 = f32[4,1,128,128]{2,3,1,0:T(8,128)} custom-call(f32[4,1,128,128]{3,2,1,0:T(8,128)} %get-tuple-element.192), custom_call_target="InvertDiagBlocksLowerTriangular" | custom-call | tf_op jit(solution)/shard_map/vmap(jit(_cho_solve))/triangular_solve/custom-call.2 | solution.py:19
  1047.0 9.4 fusion.284
  1067.4 40.8 %custom-call.129 = f32[4,1,128,128]{2,3,1,0:T(8,128)} custom-call(f32[4,1,128,128]{3,2,1,0:T(8,128)} %get-tuple-element.167), custom_call_target="InvertDiagBlocksLowerTriangular" | custom-call | tf_op jit(solution)/shard_map/transpose(jvp(vmap(jit(cholesky))))/triangular_solve/custom-call.2 | solution.py:18
  1108.2 40.7 %custom-call.156 = f32[4,1,128,128]{2,3,1,0:T(8,128)} custom-call(f32[4,1,128,128]{3,2,1,0:T(8,128)} %get-tuple-element.191), custom_call_target="InvertDiagBlocksLowerTriangular" | custom-call | tf_op jit(solution)/shard_map/transpose(jvp(vmap(jit(cholesky))))/triangular_solve/custom-call.2 | solution.py:18
  1149.0 40.7 %custom-call.120 = f32[4,1,128,128]{2,3,1,0:T(8,128)} custom-call(f32[4,1,128,128]{3,2,1,0:T(8,128)} %get-tuple-element.197), custom_call_target="InvertDiagBlocksLowerTriangular" | custom-call | tf_op jit(solution)/shard_map/transpose(jvp(vmap(jit(cholesky))))/triangular_solve/custom-call.2 | solution.py:18
  1189.7 40.7 %custom-call.147 = f32[4,1,128,128]{2,3,1,0:T(8,128)} custom-call(f32[4,1,128,128]{3,2,1,0:T(8,128)} %get-tuple-element.199), custom_call_target="InvertDiagBlocksLowerTriangular" | custom-call | tf_op jit(solution)/shard_map/transpose(jvp(vmap(jit(cholesky))))/triangular_solve/custom-call.2 | solution.py:18
  1230.5 41.1 %custom-call.138 = f32[4,1,128,128]{2,3,1,0:T(8,128)} custom-call(f32[4,1,128,128]{3,2,1,0:T(8,128)} %get-tuple-element.201), custom_call_target="InvertDiagBlocksLowerTriangular" | custom-call | tf_op jit(solution)/shard_map/transpose(jvp(vmap(jit(cholesky))))/triangular_solve/custom-call.2 | solution.py:18
  1509.0 11.5 fusion.283
  1523.1 52.6 %all-gather.20.cloned.1.call-done = f32[32,128,128]{2,1,0:T(8,128)} async-done(((f32[4,128,128]{2,1,0:T(8,128)}), f32[32,128,128]{2,1,0:T(8,128)}) %all-gather.20.cloned.1.call-update) | async-done | bytes 2097168 | tf_op jit(solution)/shard_map/all_gather | solution.py:59
  1577.4 52.4 %all-gather.18.cloned.1.call-done = f32[32,128,128]{2,1,0:T(8,128)} async-done(((f32[4,128,128]{2,1,0:T(8,128)}), f32[32,128,128]{2,1,0:T(8,128)}) %all-gather.18.cloned.1.call-update) | async-done | bytes 2097168 | tf_op jit(solution)/shard_map/all_gather | solution.py:59
  1631.6 52.4 %all-gather.16.cloned.1.call-done = f32[32,128,128]{2,1,0:T(8,128)} async-done(((f32[4,128,128]{2,1,0:T(8,128)}), f32[32,128,128]{2,1,0:T(8,128)}) %all-gather.16.cloned.1.call-update) | async-done | bytes 2097168 | tf_op jit(solution)/shard_map/all_gather | solution.py:59
  1685.7 52.4 %all-gather.14.cloned.1.call-done = f32[32,128,128]{2,1,0:T(8,128)} async-done(((f32[4,128,128]{2,1,0:T(8,128)}), f32[32,128,128]{2,1,0:T(8,128)}) %all-gather.14.cloned.1.call-update) | async-done | bytes 2097168 | tf_op jit(solution)/shard_map/all_gather | solution.py:59
  1741.6 179.6 %reduce-scatter.2.cloned.1.call-done = f32[512,512]{1,0:T(8,128)} async-done(((f32[512,8192]{1,0:T(8,128)}), f32[512,512]{1,0:T(8,128)}) %reduce-scatter.2.cloned.1.call-update) | async-done | bytes 1048592 | tf_op jit(solution)/shard_map/reduce_scatter | solution.py:89
  (384 shorter events, 415.7 us)
Async XLA Ops:
  7.2 553.8 %copy-start = (bf16[512,512]{1,0:T(8,128)(2,1)S(1)}, bf16[512,512]{1,0:T(8,128)(2,1)}, u32[]{:S(2)}) copy-start(bf16[512,512]{1,0:T(8,128)(2,1)} %param.24) | copy-start | bytes 1572868
  7.2 1039.8 %all-gather.12.cloned.1.call-start = ((), (), s32[]{:S(2)}) async-start(), calls=%async_computation.2 | async-start | bytes 8912896 | tf_op jit(solution)/shard_map/all_gather | solution.py:91
  7.9 1513.5 %all-gather.22.cloned.1.call-start = ((), (), s32[]{:S(2)}) async-start(), calls=%async_computation.7 | async-start | bytes 2359296 | tf_op jit(solution)/shard_map/all_gather | solution.py:59
  313.6 245.9 %copy-start.35 = (f32[4,128,128]{2,1,0:T(8,128)}, f32[4,128,128]{2,1,0:T(8,128)S(1)}, u32[]{:S(2)}) copy-start(f32[4,128,128]{2,1,0:T(8,128)S(1)} %custom-call.113) | copy-start | bytes 786436
  366.8 195.8 %copy-start.37 = (f32[4,128,128]{2,1,0:T(8,128)}, f32[4,128,128]{2,1,0:T(8,128)S(1)}, u32[]{:S(2)}) copy-start(f32[4,128,128]{2,1,0:T(8,128)S(1)} %custom-call.131) | copy-start | bytes 786436
  414.6 145.4 %copy-start.36 = (f32[4,128,128]{2,1,0:T(8,128)}, f32[4,128,128]{2,1,0:T(8,128)S(1)}, u32[]{:S(2)}) copy-start(f32[4,128,128]{2,1,0:T(8,128)S(1)} %custom-call.122) | copy-start | bytes 786436
  465.3 54.0 %copy-start.39 = (f32[4,128,128]{2,1,0:T(8,128)}, f32[4,128,128]{2,1,0:T(8,128)S(1)}, u32[]{:S(2)}) copy-start(f32[4,128,128]{2,1,0:T(8,128)S(1)} %custom-call.149) | copy-start | bytes 786436
  559.9 53.8 %copy-start.24 = (f32[4,128,128]{2,1,0:T(8,128)}, f32[4,128,128]{2,1,0:T(8,128)S(1)}, u32[]{:S(2)}) copy-start(f32[4,128,128]{2,1,0:T(8,128)S(1)} %fusion.180) | copy-start | bytes 786436
  569.8 90.8 %collective-permute-start = (f32[512,4,64]{0,2,1:T(8,128)}, f32[512,4,64]{0,2,1:T(8,128)}, u32[]{:S(2)}, u32[]{:S(2)}) collective-permute-start(f32[512,4,64]{0,2,1:T(8,128)} %copy.594), channel_id=1, source_target_pairs={{0,1},{1,0},{2,3},{3,2},{4,5},{5,4},{6,7},{7,6},{8,9},{9,8},{10,11... | collective-permute-start | bytes 1572872 | tf_op jit(solution)/shard_map/ppermute | solution.py:8
  612.1 52.6 %copy-start.25 = (f32[4,128,128]{2,1,0:T(8,128)}, f32[4,128,128]{2,1,0:T(8,128)S(1)}, u32[]{:S(2)}) copy-start(f32[4,128,128]{2,1,0:T(8,128)S(1)} %fusion.200) | copy-start | bytes 786436
  616.2 56.5 %copy-start.23 = (f32[4,128,128]{2,1,0:T(8,128)}, f32[4,128,128]{2,1,0:T(8,128)S(1)}, u32[]{:S(2)}) copy-start(f32[4,128,128]{2,1,0:T(8,128)S(1)} %fusion.185) | copy-start | bytes 786436
  671.5 127.0 %collective-permute-start.1 = (f32[512,4,64]{0,2,1:T(8,128)}, f32[512,4,64]{0,2,1:T(8,128)}, u32[]{:S(2)}, u32[]{:S(2)}) collective-permute-start(f32[512,4,64]{0,2,1:T(8,128)} %copy.598), channel_id=1, source_target_pairs={{0,1},{1,0},{2,3},{3,2},{4,5},{5,4},{6,7},{7,6},{8,9},{9,8},{10,11... | collective-permute-start | bytes 1572872 | tf_op jit(solution)/shard_map/ppermute | solution.py:8
  805.6 47.6 %collective-permute-start.2 = (f32[512,4,64]{0,2,1:T(8,128)S(1)}, f32[512,4,64]{0,2,1:T(8,128)}, u32[]{:S(2)}, u32[]{:S(2)}) collective-permute-start(f32[512,4,64]{0,2,1:T(8,128)S(1)} %copy.601), channel_id=1, source_target_pairs={{0,2},{1,3},{2,0},{3,1},{4,6},{5,7},{6,4},{7,5},{8,10},{9,11},{10,... | collective-permute-start | bytes 1572872 | tf_op jit(solution)/shard_map/ppermute | solution.py:8
  862.8 128.4 %collective-permute-start.3 = (f32[512,4,64]{0,2,1:T(8,128)}, f32[512,4,64]{0,2,1:T(8,128)}, u32[]{:S(2)}, u32[]{:S(2)}) collective-permute-start(f32[512,4,64]{0,2,1:T(8,128)} %copy.605), channel_id=1, source_target_pairs={{0,2},{1,3},{2,0},{3,1},{4,6},{5,7},{6,4},{7,5},{8,10},{9,11},{10,... | collective-permute-start | bytes 1572872 | tf_op jit(solution)/shard_map/ppermute | solution.py:8
  998.4 14.5 collective-permute-start.4
  1022.4 13.6 collective-permute-start.5
  1043.9 228.3 %collective-permute-start.6 = (f32[512,4,64]{0,2,1:T(8,128)}, f32[512,4,64]{0,2,1:T(8,128)}, u32[]{:S(2)}, u32[]{:S(2)}) collective-permute-start(f32[512,4,64]{0,2,1:T(8,128)} %copy.615), channel_id=1, source_target_pairs={{0,8},{1,9},{2,10},{3,11},{4,12},{5,13},{6,14},{7,15},{8,0},{9,1},... | collective-permute-start | bytes 1572872 | tf_op jit(solution)/shard_map/ppermute | solution.py:8
  1065.6 212.0 %collective-permute-start.8 = (f32[512,4,64]{0,2,1:T(8,128)}, f32[512,4,64]{0,2,1:T(8,128)}, u32[]{:S(2)}, u32[]{:S(2)}) collective-permute-start(f32[512,4,64]{0,2,1:T(8,128)} %copy.628), channel_id=1, source_target_pairs={{0,8},{1,9},{2,10},{3,11},{4,12},{5,13},{6,14},{7,15},{8,0},{9,1},... | collective-permute-start | bytes 1572872 | tf_op jit(solution)/shard_map/ppermute | solution.py:8
  1067.4 212.6 %copy-start.15 = (f32[512,1,4,64]{3,0,2,1:T(8,128)S(1)}, f32[512,1,4,64]{3,0,2,1:T(8,128)}, u32[]{:S(2)}) copy-start(f32[512,1,4,64]{3,0,2,1:T(8,128)} %copy.861) | copy-start | bytes 1572868
  1288.5 17.0 collective-permute-start.9
  1312.6 11.5 collective-permute-start.10
  1337.4 10.6 collective-permute-start.11
  1356.0 9.8 collective-permute-start.12
  1381.2 9.5 collective-permute-start.13
  1398.8 7.6 collective-permute-start.14
  1425.0 9.3 collective-permute-start.15
  1466.3 109.4 %all-gather.20.cloned.1.call-start = ((), (), s32[]{:S(2)}) async-start(), calls=%async_computation.6 | async-start | bytes 2359296 | tf_op jit(solution)/shard_map/all_gather | solution.py:59
  1473.2 156.6 %all-gather.18.cloned.1.call-start = ((), (), s32[]{:S(2)}) async-start(), calls=%async_computation.5 | async-start | bytes 2359296 | tf_op jit(solution)/shard_map/all_gather | solution.py:59
  1482.3 201.7 %all-gather.16.cloned.1.call-start = ((), (), s32[]{:S(2)}) async-start(), calls=%async_computation.4 | async-start | bytes 2359296 | tf_op jit(solution)/shard_map/all_gather | solution.py:59
  1490.4 247.8 %all-gather.14.cloned.1.call-start = ((), (), s32[]{:S(2)}) async-start(), calls=%async_computation.3 | async-start | bytes 2359296 | tf_op jit(solution)/shard_map/all_gather | solution.py:59
  1494.9 426.3 %reduce-scatter.2.cloned.1.call-start = ((), (), s32[]{:S(2)}) async-start(), calls=%async_computation.1 | async-start | bytes 17825792 | tf_op jit(solution)/shard_map/reduce_scatter | solution.py:89
  1497.8 10.1 collective-permute-start.7
  (34 other events, 291.8 us)
Sparse Core Ops, SparseCore 0:
  9.7 54.5 all-gather.11
  1466.4 54.9 all-gather.21
  1523.8 51.8 all-gather.19
  1577.9 51.8 all-gather.17
  1632.0 51.8 all-gather.15
  1686.2 51.8 all-gather.13
  1741.1 180.0 reduce-scatter.1
